TPU v7x, 32 devices: a whole 2x2x4 slice. The times are simulated.
32 devices in a mesh: row: 4 (over z), col: 8 (over y, x, core).
Axes of the slice: x: 2, y: 2, z: 4, core: 2. Of those that a mesh axis runs over, the one named last changes fastest.
Arguments:
- tokens: bfloat16 [512, 8192], P('col', 'row'), may hold values from -6 to 6
- modality: int32 [512], P('row'), may hold values 0 or 1
- in_weight: bfloat16 [8192, 2, 28672], P('row', None, 'col'), may hold values from -0.0625 to 0.0625
- down_weight: bfloat16 [28672, 8192], P('col', 'row'), may hold values from -0.03125 to 0.03125
- d_mixed: bfloat16 [512, 8192], P('col', 'row'), may hold values from -6 to 6
Outputs:
- mixed: bfloat16 [512, 8192], P('col', 'row')
- d_down: bfloat16 [28672, 8192], P('col', 'row')
- d_in: bfloat16 [8192, 2, 28672], P('row', None, 'col')
- d_tokens: bfloat16 [512, 8192], P('col', 'row')
All inputs are finite; a program needn't handle non-finite values. No bound on the sum of `modality` on one device may be relied on, other than what follows from the above.
Results may differ from a plain program's by a relative error of at most 0.0049.
Values may be sent and summed in bfloat16 or wider, within the bound.
A program may use at most 192 MiB of HBM per device.

v0:
```python
import functools

import jax
import jax.numpy as jnp
from jax import lax
from jax.experimental import pallas as pl
from jax.experimental.pallas import tpu as pltpu
from jax.sharding import PartitionSpec as P

MESH = pl.DeviceIdType.MESH
OVER_LAST = (((1,), (1,)), ((), ()))
OVER_FIRST = (((0,), (0,)), ((), ()))


def dot(a, b, dims=(((1,), (0,)), ((), ()))):
    return lax.dot_general(a, b, dims, preferred_element_type=jnp.float32)


def exchange(partial, axis):
    count = lax.axis_size(axis)
    me = lax.axis_index(axis)
    rows = partial.shape[0] // count
    received = []
    for shift in range(1, count):
        start = lax.rem(me + shift, count) * rows
        block = lax.dynamic_slice_in_dim(partial, start, rows, 0).astype(jnp.bfloat16)
        moves = [(i, (i + shift) % count) for i in range(count)]
        received.append(lax.ppermute(block, axis, moves))
    total = lax.dynamic_slice_in_dim(partial, me * rows, rows, 0)
    for block in received:
        total = total + block.astype(jnp.float32)
    return total


def paired_columns(rows_ref, gate_ref, up_ref, out_ref):
    for part, side_ref in enumerate((gate_ref, up_ref)):
        out_ref[:, part, :] = dot(rows_ref[...], side_ref[...], OVER_FIRST).astype(jnp.bfloat16)


def in_gradient(rows, d_projected):
    count, depth = rows.shape
    width = d_projected.shape[1] // 2
    deep = depth // 8
    wide = max(w for w in range(128, 2049, 128) if width % w == 0)
    return pl.pallas_call(
        paired_columns,
        grid=(width // wide, depth // deep),
        in_specs=[
            pl.BlockSpec((count, deep), lambda j, i: (0, i)),
            pl.BlockSpec((count, wide), lambda j, i: (0, j)),
            pl.BlockSpec((count, wide), lambda j, i: (0, j + width // wide)),
        ],
        out_specs=pl.BlockSpec((deep, 2, wide), lambda j, i: (i, 0, j)),
        out_shape=jax.ShapeDtypeStruct((depth, 2, width), jnp.bfloat16),
        cost_estimate=pl.CostEstimate(
            flops=4 * count * depth * width,
            bytes_accessed=4 * (depth * width + count * width + count * depth),
            transcendentals=0,
        ),
    )(rows, d_projected, d_projected)


def swiglu_terms(gate, up, d_hidden):
    sig = jax.nn.sigmoid(gate)
    activated = gate * sig
    d_gate = d_hidden * up * (sig + gate * sig * (1.0 - sig))
    return activated * up, d_gate, d_hidden * activated


def block_terms(rows, cotangents, in_weight, down_weight):
    width = in_weight.shape[2]
    flat_in = in_weight.reshape(in_weight.shape[0], -1)
    d_hidden = exchange(dot(cotangents, down_weight, OVER_LAST), "row")
    projected = exchange(dot(rows, flat_in), "row")
    hidden, d_gate, d_up = swiglu_terms(projected[:, :width], projected[:, width:], d_hidden)
    d_local = jnp.concatenate([d_gate, d_up], 1).astype(jnp.bfloat16)
    hidden_all = lax.all_gather(hidden.astype(jnp.bfloat16), "row", axis=0, tiled=True)
    d_projected = lax.all_gather(d_local, "row", axis=0, tiled=True)
    mixed = exchange(dot(hidden_all, down_weight), "col").astype(jnp.bfloat16)
    d_down = dot(hidden_all, cotangents, OVER_FIRST).astype(jnp.bfloat16)
    d_tokens = exchange(dot(d_projected, flat_in, OVER_LAST), "col").astype(jnp.bfloat16)
    return (mixed, d_down, in_gradient(rows, d_projected), d_tokens)


def chain_kernel(
    size, units, wide, rows_ref, cots_ref, in_ref, down_ref, mixed_ref, d_tokens_ref, terms_ref,
    raw, w_down, w_in, partial, sums, terms,
    load_sem, sum_send, sum_recv, term_send, term_recv, out_sem,
):
    z = lax.axis_index("row")
    middle = size // 2
    slots = w_down.shape[0]
    held = partial.shape[0]
    near = jnp.minimum(z, size - 1 - z)
    last_lag = 2 * middle + 1 - near

    def owner_of(u):
        return middle - 1 + lax.rem(u, 2)

    def loads(u):
        columns = pl.ds(pl.multiple_of(u * wide, wide), wide)
        slot = lax.rem(u, 2)
        return (
            pltpu.make_async_copy(in_ref.at[:, :, columns], raw.at[slot], load_sem.at[0, slot]),
            pltpu.make_async_copy(down_ref.at[columns, :], w_down.at[lax.rem(u, slots)], load_sem.at[1, slot]),
        )

    def sum_copy(u, side):
        return pltpu.make_async_remote_copy(
            src_ref=sums.at[side, u], dst_ref=sums.at[side, u],
            send_sem=sum_send.at[u], recv_sem=sum_recv.at[side, u],
            device_id={"row": z + 1 - 2 * side}, device_id_type=MESH,
        )

    def term_copy(u, side):
        return pltpu.make_async_remote_copy(
            src_ref=terms.at[u], dst_ref=terms.at[u],
            send_sem=term_send.at[side, u], recv_sem=term_recv.at[u],
            device_id={"row": z + 1 - 2 * side}, device_id_type=MESH,
        )

    def out_copy(u):
        columns = pl.ds(pl.multiple_of(u * 3 * wide, wide), 3 * wide)
        return pltpu.make_async_copy(terms.at[u], terms_ref.at[:, columns], out_sem.at[u])

    barrier = pltpu.get_barrier_semaphore()
    for step in (-1, 1):
        @pl.when((z + step >= 0) & (z + step < size))
        def _():
            pl.semaphore_signal(barrier, inc=1, device_id={"row": z + step}, device_id_type=MESH)
    for copy in loads(0):
        copy.start()
    mixed_ref[...] = jnp.zeros_like(mixed_ref)
    d_tokens_ref[...] = jnp.zeros_like(d_tokens_ref)
    pl.semaphore_wait(barrier, jnp.where(near > 0, 2, 1))

    @pl.loop(0, units + 2 * middle + 1)
    def _(t):
        @pl.when(t < units)
        def _():
            for copy in loads(t):
                copy.wait()

            @pl.when(t + 1 < units)
            def _():
                for copy in loads(t + 1):
                    copy.start()

            slot, here = lax.rem(t, slots), lax.rem(t, held)
            for part in range(2):
                w_in[slot, :, part * wide:(part + 1) * wide] = raw[lax.rem(t, 2), :, part, :]
            partial[here, :, :2 * wide] = dot(rows_ref[...], w_in[slot])
            partial[here, :, 2 * wide:] = dot(cots_ref[...], w_down[slot], OVER_LAST)

        relayed = t - near

        @pl.when((relayed >= 0) & (relayed < units) & (owner_of(relayed) != z))
        def _():
            side = jnp.where(z < owner_of(relayed), 0, 1)
            here = lax.rem(relayed, held)

            @pl.when(near > 0)
            def _():
                sum_copy(relayed, side).wait_recv()
                sums[side, relayed] = (
                    partial[here] + sums[side, relayed].astype(jnp.float32)
                ).astype(sums.dtype)

            @pl.when(near == 0)
            def _():
                sums[side, relayed] = partial[here].astype(sums.dtype)

            sum_copy(relayed, side).start()

        closed = t - middle

        @pl.when((closed >= 0) & (closed < units) & (owner_of(closed) == z))
        def _():
            here = lax.rem(closed, held)

            @pl.when(z > 0)
            def _():
                sum_copy(closed, 0).wait_recv()
                partial[here] += sums[0, closed].astype(jnp.float32)

            @pl.when(z < size - 1)
            def _():
                sum_copy(closed, 1).wait_recv()
                partial[here] += sums[1, closed].astype(jnp.float32)

            whole = partial[here]
            results = swiglu_terms(*(whole[:, k * wide:(k + 1) * wide] for k in range(3)))
            for k, result in enumerate(results):
                terms[closed, :, k * wide:(k + 1) * wide] = result.astype(jnp.bfloat16)

            @pl.when(z < size - 1)
            def _():
                term_copy(closed, 0).start()

            @pl.when(z > 0)
            def _():
                term_copy(closed, 1).start()

        used = t - last_lag

        @pl.when((used >= 0) & (used < units))
        def _():
            owner = owner_of(used)

            @pl.when(owner != z)
            def _():
                side = jnp.where(z < owner, 1, 0)
                term_copy(used, side).wait_recv()

                @pl.when(near > 0)
                def _():
                    term_copy(used, side).start()

            out_copy(used).start()
            slot = lax.rem(used, slots)
            mixed_ref[...] += dot(terms[used, :, :wide], w_down[slot])
            d_tokens_ref[...] += dot(terms[used, :, wide:], w_in[slot], OVER_LAST)

    @pl.loop(0, units)
    def _(u):
        owner = owner_of(u)
        out_copy(u).wait()

        @pl.when(owner != z)
        def _():
            sum_copy(u, jnp.where(z < owner, 0, 1)).wait_send()

            @pl.when(near > 0)
            def _():
                term_copy(u, jnp.where(z < owner, 1, 0)).wait_send()

        @pl.when(owner == z)
        def _():
            @pl.when(z < size - 1)
            def _():
                term_copy(u, 0).wait_send()

            @pl.when(z > 0)
            def _():
                term_copy(u, 1).wait_send()


def chain(rows, cotangents, in_weight, down_weight, collective_id):
    size = lax.axis_size("row")
    count, depth = rows.shape
    width = down_weight.shape[0]
    wide = 128
    units = width // wide
    slots = 2 * (size // 2) + 4
    held = size // 2 + 1
    sum_type = jnp.bfloat16 if size <= 4 else jnp.float32
    vmem, hbm = pl.BlockSpec(memory_space=pltpu.VMEM), pl.BlockSpec(memory_space=pl.ANY)
    dma = pltpu.SemaphoreType.DMA
    return pl.pallas_call(
        functools.partial(chain_kernel, size, units, wide),
        in_specs=[vmem, vmem, hbm, hbm],
        out_specs=[vmem, vmem, hbm],
        out_shape=[
            jax.ShapeDtypeStruct((count, depth), jnp.float32),
            jax.ShapeDtypeStruct((count, depth), jnp.float32),
            jax.ShapeDtypeStruct((count, 3 * width), jnp.bfloat16),
        ],
        scratch_shapes=[
            pltpu.VMEM((2, depth, 2, wide), jnp.bfloat16),
            pltpu.VMEM((slots, wide, depth), jnp.bfloat16),
            pltpu.VMEM((slots, depth, 2 * wide), jnp.bfloat16),
            pltpu.VMEM((held, count, 3 * wide), jnp.float32),
            pltpu.VMEM((2, units, count, 3 * wide), sum_type),
            pltpu.VMEM((units, count, 3 * wide), jnp.bfloat16),
            dma((2, 2)), dma((units,)), dma((2, units)), dma((2, units)), dma((units,)), dma((units,)),
        ],
        compiler_params=pltpu.CompilerParams(
            collective_id=collective_id, has_side_effects=True, vmem_limit_bytes=60 * 1024 * 1024
        ),
        cost_estimate=pl.CostEstimate(
            flops=12 * count * depth * width, bytes_accessed=6 * depth * width, transcendentals=count * width
        ),
    )(rows, cotangents, in_weight, down_weight)


def weight_kernel(group, wide, rows_ref, cots_ref, terms_ref, d_in_ref, d_down_ref):
    for g in range(group):
        columns = slice(g * wide, (g + 1) * wide)
        base = 3 * g * wide
        d_down_ref[columns, :] = dot(
            terms_ref[:, base:base + wide], cots_ref[...], OVER_FIRST
        ).astype(jnp.bfloat16)
        both = dot(rows_ref[...], terms_ref[:, base + wide:base + 3 * wide], OVER_FIRST).astype(jnp.bfloat16)
        for part in range(2):
            d_in_ref[:, part, columns] = both[:, part * wide:(part + 1) * wide]


def weight_gradients(rows, cotangents, terms):
    count, depth = rows.shape
    wide = 128
    width = terms.shape[1] // 3
    units = width // wide
    group = 2 if units % 2 == 0 else 1
    return pl.pallas_call(
        functools.partial(weight_kernel, group, wide),
        grid=(units // group,),
        in_specs=[
            pl.BlockSpec((count, depth), lambda j: (0, 0)),
            pl.BlockSpec((count, depth), lambda j: (0, 0)),
            pl.BlockSpec((count, 3 * group * wide), lambda j: (0, j)),
        ],
        out_specs=[
            pl.BlockSpec((depth, 2, group * wide), lambda j: (0, 0, j)),
            pl.BlockSpec((group * wide, depth), lambda j: (j, 0)),
        ],
        out_shape=[
            jax.ShapeDtypeStruct((depth, 2, width), jnp.bfloat16),
            jax.ShapeDtypeStruct((width, depth), jnp.bfloat16),
        ],
        cost_estimate=pl.CostEstimate(
            flops=6 * count * depth * width,
            bytes_accessed=6 * depth * width + 6 * count * width + 4 * count * depth,
            transcendentals=0,
        ),
    )(rows, cotangents, terms)


def per_device(tokens, modality, in_weight, down_weight, d_mixed):
    every = lambda x: lax.all_gather(x, "col", axis=0, tiled=True)
    rows_all = every(tokens)
    cots_all = every(d_mixed)
    chosen = lax.all_gather(modality, "row", axis=0, tiled=True) == 1
    total = chosen.shape[0]
    place = jnp.cumsum(chosen.astype(jnp.int32)) - 1
    packed = total * 9 // 16

    def packed_form(rows, cotangents, w_in, w_down):
        pick = (chosen[None, :] & (place[None, :] == jnp.arange(packed)[:, None])).astype(jnp.bfloat16)
        take = lambda x: dot(pick, x).astype(jnp.bfloat16)
        spread = lambda x: dot(pick, x.astype(jnp.bfloat16), OVER_FIRST)
        rows, cotangents = take(rows), take(cotangents)
        mixed, d_tokens, terms = chain(rows, cotangents, w_in, w_down, 1)
        d_in, d_down = weight_gradients(rows, cotangents, terms)
        mixed = exchange(spread(mixed), "col").astype(jnp.bfloat16)
        d_tokens = exchange(spread(d_tokens), "col").astype(jnp.bfloat16)
        return (mixed, d_down, d_in, d_tokens)

    def whole_form(rows, cotangents, w_in, w_down):
        keep = chosen[:, None].astype(jnp.bfloat16)
        return block_terms(rows * keep, cotangents * keep, w_in, w_down)

    return lax.cond(
        place[-1] < packed, packed_form, whole_form, rows_all, cots_all, in_weight, down_weight
    )


def solution(mesh):
    return jax.shard_map(
        per_device,
        mesh=mesh,
        in_specs=(
            P("col", "row"),
            P("row"),
            P("row", None, "col"),
            P("col", "row"),
            P("col", "row"),
        ),
        out_specs=(P("col", "row"), P("col", "row"), P("row", None, "col"), P("col", "row")),
        check_vma=False,
    )
```

profile of v0, /device:TPU:0, one launch (start us, length us, event | category | flops | bytes accessed | tf_op | source)
XLA Modules:
  0.0 403.4 jit_solution(13562071478566607294)
XLA Ops:
  8.6 12.8 %all-gather = s32[4,1,128]{2,1,0:T(1,128)S(1)} all-gather(s32[1,1,128]{2,1,0:T(1,128)} %bitcast.25), channel_id=1, replica_groups=mesh['row'=4,'col'=8] {'row'}, dimensions={0}, use_global_device_ids=true | all-gather | bytes 2560 | tf_op jit(solution)/shard_map/all_gather | solution.py:332
  23.3 17.1 %all-gather.10.cloned.1.call-done = bf16[512,2048]{1,0:T(8,128)(2,1)} async-done(((bf16[64,2048]{1,0:T(8,128)(2,1)}), bf16[512,2048]{1,0:T(8,128)(2,1)}) %all-gather.10.cloned.1.call-update) | async-done | bytes 2097168 | tf_op jit(solution)/shard_map/all_gather | solution.py:329
  40.4 29.7 %all-gather.12.cloned.1.call-done = bf16[512,2048]{1,0:T(8,128)(2,1)} async-done(((bf16[64,2048]{1,0:T(8,128)(2,1)}), bf16[512,2048]{1,0:T(8,128)(2,1)}) %all-gather.12.cloned.1.call-update) | async-done | bytes 2097168 | tf_op jit(solution)/shard_map/all_gather | solution.py:329
  70.1 325.4 %conditional.4 = (bf16[3584,2048]{1,0:T(8,128)(2,1)}, bf16[2048,2,3584]{2,1,0:T(2,128)(2,1)}, bf16[64,2048]{1,0:T(8,128)(2,1)S(1)}, bf16[64,2048]{1,0:T(8,128)(2,1)S(1)}) conditional(s32[]{:T(128)} %bitcast.3, (pred[512]{0:T(512)(128)(4,1)S(1)}, bf16[512,2048]{1,0:T(8,128)(2,1)}, bf16[2048,2,3584]{2,1,0:T(2,128)(2,1)}, bf16[512,2048]{1,0:T(8,128)(2,1)}, ...), branch_computations={%region_2.3_spmd, %region_3.4_spmd} | conditional | flops 67678502912 | bytes 516823200
  77.3 3.5 convolution_convert_fusion.2.rows_ref
  80.9 1.8 convolution_convert_fusion.1.cots_ref
  82.7 174.8 %branch_1_fun.2 = (f32[288,2048]{1,0:T(8,128)}, f32[288,2048]{1,0:T(8,128)}, bf16[288,10752]{1,0:T(8,128)(2,1)}) custom-call(bf16[288,2048]{1,0:T(8,128)(2,1)} %convolution_convert_fusion.2.rows_ref, bf16[288,2048]{1,0:T(8,128)(2,1)} %convolution_convert_fusion.1.cots_ref, bf16[2048,2,3584]{2,1,0:T(2,128)(2,1)} %get-tuple-element.47.in_ref, ...), custom_call_target="tpu_custom_call" | custom-call | flops 25367150592 | bytes 44040192 | tf_op jit(solution)/shard_map/cond/branch_1_fun/pallas_call | solution.py:259
  257.5 5.0 %fusion.5 = f32[512,2048]{1,0:T(8,128)} fusion(f32[288,2048]{1,0:T(8,128)} %get-tuple-element.53, s32[512]{0:T(512)S(1)} %get-tuple-element.44, pred[512]{0:T(512)(128)(4,1)S(1)} %get-tuple-element.43), kind=kOutput, calls=%fused_computation.39 | convolution fusion | flops 604864512 | bytes 6556160 | tf_op jit(solution)/shard_map/cond/branch_1_fun/dot_general | solution.py:16
  262.5 3.1 dynamic-slice_convert_fusion.26
  265.6 2.6 collective-permute-start.33
  272.1 2.0 copy-done
  275.1 1.5 collective-permute-start.29
  276.5 1.9 collective-permute-start.28
  278.4 3.7 collective-permute-done.32
  282.1 2.9 collective-permute-done.31
  285.1 3.3 collective-permute-start.26
  288.3 81.6 %branch_1_fun.3 = (bf16[2048,2,3584]{2,1,0:T(2,128)(2,1)}, bf16[3584,2048]{1,0:T(8,128)(2,1)}) custom-call(bf16[288,2048]{1,0:T(8,128)(2,1)} %convolution_convert_fusion.2.rows_ref, bf16[288,2048]{1,0:T(8,128)(2,1)} %convolution_convert_fusion.1.cots_ref, bf16[288,10752]{1,0:T(8,128)(2,1)} %get-tuple-element.49.terms_ref), custom_call_target="tpu_custom_call" | custom-call | flops 12683575296 | bytes 52592640 | tf_op jit(solution)/shard_map/cond/branch_1_fun/pallas_call | solution.py:304
  370.3 2.0 collective-permute-start.24
  372.7 1.4 collective-permute-start.22
  374.1 2.9 collective-permute-start.21
  377.0 2.2 add_convert_fusion.2
  379.2 3.3 collective-permute-done.24
  382.5 9.4 %collective-permute-done.23 = bf16[64,2048]{1,0:T(8,128)(2,1)S(1)} collective-permute-done((bf16[64,2048]{1,0:T(8,128)(2,1)S(1)}, bf16[64,2048]{1,0:T(8,128)(2,1)S(1)}, u32[]{:S(2)}, u32[]{:S(2)}) %collective-permute-start.23) | collective-permute-done | bytes 262176 | tf_op jit(solution)/shard_map/cond/branch_1_fun/ppermute | solution.py:28
  391.9 1.9 collective-permute-done.22
  (42 shorter events, 10.5 us)
Async XLA Ops:
  7.2 33.2 %all-gather.10.cloned.1.call-start = ((), (), s32[]{:S(2)}) async-start(), calls=%async_computation.2 | async-start | bytes 2359296 | tf_op jit(solution)/shard_map/all_gather | solution.py:329
  7.9 62.2 %all-gather.12.cloned.1.call-start = ((), (), s32[]{:S(2)}) async-start(), calls=%async_computation.3 | async-start | bytes 2359296 | tf_op jit(solution)/shard_map/all_gather | solution.py:329
  77.3 3.5 copy-start.15
  262.5 8.3 %copy-start.2 = (f32[288,2048]{1,0:T(8,128)S(1)}, f32[288,2048]{1,0:T(8,128)}, u32[]{:S(2)}) copy-start(f32[288,2048]{1,0:T(8,128)} %get-tuple-element.52) | copy-start | bytes 7077892
  265.6 9.5 %collective-permute-start.27 = (bf16[64,2048]{1,0:T(8,128)(2,1)S(1)}, bf16[64,2048]{1,0:T(8,128)(2,1)S(1)}, u32[]{:S(2)}, u32[]{:S(2)}) collective-permute-start(bf16[64,2048]{1,0:T(8,128)(2,1)S(1)} %get-tuple-element.97), channel_id=1, source_target_pairs={{0,1},{1,2},{2,3},{3,4},{4,5},{5,6},{6,7},{7,0},{8,9},{9,10},{10,1... | collective-permute-start | bytes 786440 | tf_op jit(solution)/shard_map/cond/branch_1_fun/ppermute | solution.py:28
  265.6 10.9 %collective-permute-start.33 = (bf16[64,2048]{1,0:T(8,128)(2,1)S(1)}, bf16[64,2048]{1,0:T(8,128)(2,1)S(1)}, u32[]{:S(2)}, u32[]{:S(2)}) collective-permute-start(bf16[64,2048]{1,0:T(8,128)(2,1)S(1)} %get-tuple-element.98), channel_id=1, source_target_pairs={{0,7},{1,0},{2,1},{3,2},{4,3},{5,4},{6,5},{7,6},{8,15},{9,8},{10,9... | collective-permute-start | bytes 786440 | tf_op jit(solution)/shard_map/cond/branch_1_fun/ppermute | solution.py:28
  268.2 13.9 %collective-permute-start.32 = (bf16[64,2048]{1,0:T(8,128)(2,1)S(1)}, bf16[64,2048]{1,0:T(8,128)(2,1)S(1)}, u32[]{:S(2)}, u32[]{:S(2)}) collective-permute-start(bf16[64,2048]{1,0:T(8,128)(2,1)S(1)} %get-tuple-element.99), channel_id=1, source_target_pairs={{0,6},{1,7},{2,0},{3,1},{4,2},{5,3},{6,4},{7,5},{8,14},{9,15},{10,... | collective-permute-start | bytes 786440 | tf_op jit(solution)/shard_map/cond/branch_1_fun/ppermute | solution.py:28
  269.1 15.9 %collective-permute-start.31 = (bf16[64,2048]{1,0:T(8,128)(2,1)S(1)}, bf16[64,2048]{1,0:T(8,128)(2,1)S(1)}, u32[]{:S(2)}, u32[]{:S(2)}) collective-permute-start(bf16[64,2048]{1,0:T(8,128)(2,1)S(1)} %get-tuple-element.100), channel_id=1, source_target_pairs={{0,5},{1,6},{2,7},{3,0},{4,1},{5,2},{6,3},{7,4},{8,13},{9,14},{10,... | collective-permute-start | bytes 786440 | tf_op jit(solution)/shard_map/cond/branch_1_fun/ppermute | solution.py:28
  269.5 100.4 %collective-permute-start.30 = (bf16[64,2048]{1,0:T(8,128)(2,1)}, bf16[64,2048]{1,0:T(8,128)(2,1)}, u32[]{:S(2)}, u32[]{:S(2)}) collective-permute-start(bf16[64,2048]{1,0:T(8,128)(2,1)} %get-tuple-element.101), channel_id=1, source_target_pairs={{0,4},{1,5},{2,6},{3,7},{4,0},{5,1},{6,2},{7,3},{8,12},{9,13},{10,... | collective-permute-start | bytes 786440 | tf_op jit(solution)/shard_map/cond/branch_1_fun/ppermute | solution.py:28
  272.1 2.0 copy-start
  275.1 95.2 %collective-permute-start.29 = (bf16[64,2048]{1,0:T(8,128)(2,1)}, bf16[64,2048]{1,0:T(8,128)(2,1)S(1)}, u32[]{:S(2)}, u32[]{:S(2)}) collective-permute-start(bf16[64,2048]{1,0:T(8,128)(2,1)} %get-tuple-element.102), channel_id=1, source_target_pairs={{0,3},{1,4},{2,5},{3,6},{4,7},{5,0},{6,1},{7,2},{8,11},{9,12},{10,... | collective-permute-start | bytes 786440 | tf_op jit(solution)/shard_map/cond/branch_1_fun/ppermute | solution.py:28
  276.5 95.8 %collective-permute-start.28 = (bf16[64,2048]{1,0:T(8,128)(2,1)}, bf16[64,2048]{1,0:T(8,128)(2,1)}, u32[]{:S(2)}, u32[]{:S(2)}) collective-permute-start(bf16[64,2048]{1,0:T(8,128)(2,1)} %get-tuple-element.103), channel_id=1, source_target_pairs={{0,2},{1,3},{2,4},{3,5},{4,6},{5,7},{6,0},{7,1},{8,10},{9,11},{10,... | collective-permute-start | bytes 786440 | tf_op jit(solution)/shard_map/cond/branch_1_fun/ppermute | solution.py:28
  282.1 90.6 %collective-permute-start.20 = (bf16[64,2048]{1,0:T(8,128)(2,1)}, bf16[64,2048]{1,0:T(8,128)(2,1)S(1)}, u32[]{:S(2)}, u32[]{:S(2)}) collective-permute-start(bf16[64,2048]{1,0:T(8,128)(2,1)} %get-tuple-element.104), channel_id=1, source_target_pairs={{0,1},{1,2},{2,3},{3,4},{4,5},{5,6},{6,7},{7,0},{8,9},{9,10},{10,1... | collective-permute-start | bytes 786440 | tf_op jit(solution)/shard_map/cond/branch_1_fun/ppermute | solution.py:28
  285.1 89.1 %collective-permute-start.26 = (bf16[64,2048]{1,0:T(8,128)(2,1)S(1)}, bf16[64,2048]{1,0:T(8,128)(2,1)S(1)}, u32[]{:S(2)}, u32[]{:S(2)}) collective-permute-start(bf16[64,2048]{1,0:T(8,128)(2,1)S(1)} %get-tuple-element.105), channel_id=1, source_target_pairs={{0,7},{1,0},{2,1},{3,2},{4,3},{5,4},{6,5},{7,6},{8,15},{9,8},{10,9... | collective-permute-start | bytes 786440 | tf_op jit(solution)/shard_map/cond/branch_1_fun/ppermute | solution.py:28
  369.9 9.3 %collective-permute-start.25 = (bf16[64,2048]{1,0:T(8,128)(2,1)S(1)}, bf16[64,2048]{1,0:T(8,128)(2,1)S(1)}, u32[]{:S(2)}, u32[]{:S(2)}) collective-permute-start(bf16[64,2048]{1,0:T(8,128)(2,1)S(1)} %get-tuple-element.106), channel_id=1, source_target_pairs={{0,6},{1,7},{2,0},{3,1},{4,2},{5,3},{6,4},{7,5},{8,14},{9,15},{10,... | collective-permute-start | bytes 786440 | tf_op jit(solution)/shard_map/cond/branch_1_fun/ppermute | solution.py:28
  370.3 12.2 %collective-permute-start.24 = (bf16[64,2048]{1,0:T(8,128)(2,1)S(1)}, bf16[64,2048]{1,0:T(8,128)(2,1)S(1)}, u32[]{:S(2)}, u32[]{:S(2)}) collective-permute-start(bf16[64,2048]{1,0:T(8,128)(2,1)S(1)} %get-tuple-element.107), channel_id=1, source_target_pairs={{0,5},{1,6},{2,7},{3,0},{4,1},{5,2},{6,3},{7,4},{8,13},{9,14},{10,... | collective-permute-start | bytes 786440 | tf_op jit(solution)/shard_map/cond/branch_1_fun/ppermute | solution.py:28
  372.3 19.6 %collective-permute-start.23 = (bf16[64,2048]{1,0:T(8,128)(2,1)S(1)}, bf16[64,2048]{1,0:T(8,128)(2,1)S(1)}, u32[]{:S(2)}, u32[]{:S(2)}) collective-permute-start(bf16[64,2048]{1,0:T(8,128)(2,1)S(1)} %get-tuple-element.108), channel_id=1, source_target_pairs={{0,4},{1,5},{2,6},{3,7},{4,0},{5,1},{6,2},{7,3},{8,12},{9,13},{10,... | collective-permute-start | bytes 786440 | tf_op jit(solution)/shard_map/cond/branch_1_fun/ppermute | solution.py:28
  372.7 21.1 %collective-permute-start.22 = (bf16[64,2048]{1,0:T(8,128)(2,1)S(1)}, bf16[64,2048]{1,0:T(8,128)(2,1)S(1)}, u32[]{:S(2)}, u32[]{:S(2)}) collective-permute-start(bf16[64,2048]{1,0:T(8,128)(2,1)S(1)} %get-tuple-element.109), channel_id=1, source_target_pairs={{0,3},{1,4},{2,5},{3,6},{4,7},{5,0},{6,1},{7,2},{8,11},{9,12},{10,... | collective-permute-start | bytes 786440 | tf_op jit(solution)/shard_map/cond/branch_1_fun/ppermute | solution.py:28
  374.1 19.7 %collective-permute-start.21 = (bf16[64,2048]{1,0:T(8,128)(2,1)S(1)}, bf16[64,2048]{1,0:T(8,128)(2,1)S(1)}, u32[]{:S(2)}, u32[]{:S(2)}) collective-permute-start(bf16[64,2048]{1,0:T(8,128)(2,1)S(1)} %get-tuple-element.110), channel_id=1, source_target_pairs={{0,2},{1,3},{2,4},{3,5},{4,6},{5,7},{6,0},{7,1},{8,10},{9,11},{10,... | collective-permute-start | bytes 786440 | tf_op jit(solution)/shard_map/cond/branch_1_fun/ppermute | solution.py:28
  382.5 12.7 %copy-start.10 = (bf16[64,2048]{1,0:T(8,128)(2,1)S(1)}, bf16[64,2048]{1,0:T(8,128)(2,1)}, u32[]{:S(2)}) copy-start(bf16[64,2048]{1,0:T(8,128)(2,1)} %add_convert_fusion.2) | copy-start | bytes 786436
  395.5 0.7 copy-start.9
  395.5 0.8 copy-start.11
Sparse Core Ops, SparseCore 0:
  9.9 30.4 all-gather.9
  42.3 27.7 all-gather.11
where the time goes:
time: 411 us; the launch traced here: 403 us
  Pallas kernels  256 us (62%)
  waiting for transfers between devices  69.4 us (17%)
  starting transfers between devices  19 us (5%)
  between operations  15 us (4%)
  blocking collectives  12.8 us (3%)
  matrix products  11.6 us (3%)
  local copies, waits for them, and re-layouts  7.64 us (2%)
  loops' own time  7.55 us (2%)
    pallas_call x1, Pallas kernels, chain(): pl.pallas_call(functools.partial(chain_kernel, size, units, wide), in_spe...  175 us
    pallas_call x1, Pallas kernels, weight_gradients(): pl.pallas_call(functools.partial(weight_kernel, group, wide), grid=(units...  81.6 us
    all_gather x2, waiting for transfers between devices, per_device(): every = lambda x: lax.all_gather(x, 'col', axis=0, tiled=True)  46.8 us
    ppermute x14, waiting for transfers between devices, exchange(): received.append(lax.ppermute(block, axis, moves))  21.3 us
    ppermute x14, starting transfers between devices, exchange(): received.append(lax.ppermute(block, axis, moves))  18.9 us
    all_gather x1, blocking collectives, per_device(): chosen = lax.all_gather(modality, 'row', axis=0, tiled=True) == 1  12.8 us
    dot_general x4, matrix products, dot(): return lax.dot_general(a, b, dims, preferred_element_type=jnp.float32)  11.6 us
  transfers between devices with their start and end apart: 16, of which 7 were waited for; matrix products, arithmetic and copies ran while one was open for 1% of the time, Pallas kernels for 20%

commit v1 on v0

--- a/solution.py
+++ b/solution.py
@@ -37,27 +37,26 @@
         out_ref[:, part, :] = dot(rows_ref[...], side_ref[...], OVER_FIRST).astype(jnp.bfloat16)
 
 
-def in_gradient(rows, d_projected):
+def in_gradient(rows, d_gate, d_up):
     count, depth = rows.shape
-    width = d_projected.shape[1] // 2
+    width = d_gate.shape[1]
     deep = depth // 8
-    wide = max(w for w in range(128, 2049, 128) if width % w == 0)
     return pl.pallas_call(
         paired_columns,
-        grid=(width // wide, depth // deep),
+        grid=(depth // deep,),
         in_specs=[
-            pl.BlockSpec((count, deep), lambda j, i: (0, i)),
-            pl.BlockSpec((count, wide), lambda j, i: (0, j)),
-            pl.BlockSpec((count, wide), lambda j, i: (0, j + width // wide)),
+            pl.BlockSpec((count, deep), lambda i: (0, i)),
+            pl.BlockSpec((count, width), lambda i: (0, 0)),
+            pl.BlockSpec((count, width), lambda i: (0, 0)),
         ],
-        out_specs=pl.BlockSpec((deep, 2, wide), lambda j, i: (i, 0, j)),
+        out_specs=pl.BlockSpec((deep, 2, width), lambda i: (i, 0, 0)),
         out_shape=jax.ShapeDtypeStruct((depth, 2, width), jnp.bfloat16),
         cost_estimate=pl.CostEstimate(
             flops=4 * count * depth * width,
             bytes_accessed=4 * (depth * width + count * width + count * depth),
             transcendentals=0,
         ),
-    )(rows, d_projected, d_projected)
+    )(rows, d_gate, d_up)
 
 
 def swiglu_terms(gate, up, d_hidden):
@@ -79,12 +78,23 @@
     mixed = exchange(dot(hidden_all, down_weight), "col").astype(jnp.bfloat16)
     d_down = dot(hidden_all, cotangents, OVER_FIRST).astype(jnp.bfloat16)
     d_tokens = exchange(dot(d_projected, flat_in, OVER_LAST), "col").astype(jnp.bfloat16)
-    return (mixed, d_down, in_gradient(rows, d_projected), d_tokens)
+    return (mixed, d_down, in_gradient(rows, d_projected[:, :width], d_projected[:, width:]), d_tokens)
+
+
+def unpack(pairs_ref, columns_ref, apart):
+    depth, _, wide = pairs_ref.shape
+    tall = apart.shape[1] // 2
+    for step in range(depth // tall):
+        rows, buffer = slice(step * tall, (step + 1) * tall), step % apart.shape[0]
+        apart[buffer] = pairs_ref[rows].reshape(2 * tall, wide).astype(jnp.float32)
+        for part in range(2):
+            one = apart[buffer, pl.ds(part, tall, stride=2), :]
+            columns_ref[rows, part * wide:(part + 1) * wide] = one.astype(jnp.bfloat16)
 
 
 def chain_kernel(
-    size, units, wide, rows_ref, cots_ref, in_ref, down_ref, mixed_ref, d_tokens_ref, terms_ref,
-    raw, w_down, w_in, partial, sums, terms,
+    size, units, wide, rows_ref, cots_ref, in_ref, down_ref, total_ref, hidden_ref, d_gate_ref, d_up_ref,
+    raw, apart, w_down, w_in, partial, sums, terms,
     load_sem, sum_send, sum_recv, term_send, term_recv, out_sem,
 ):
     z = lax.axis_index("row")
@@ -119,9 +129,14 @@
             device_id={"row": z + 1 - 2 * side}, device_id_type=MESH,
         )
 
-    def out_copy(u):
-        columns = pl.ds(pl.multiple_of(u * 3 * wide, wide), 3 * wide)
-        return pltpu.make_async_copy(terms.at[u], terms_ref.at[:, columns], out_sem.at[u])
+    def out_copies(u):
+        columns = pl.ds(pl.multiple_of(u * wide, wide), wide)
+        return [
+            pltpu.make_async_copy(
+                terms.at[u, :, k * wide:(k + 1) * wide], ref.at[:, columns], out_sem.at[k, u]
+            )
+            for k, ref in enumerate((hidden_ref, d_gate_ref, d_up_ref))
+        ]
 
     barrier = pltpu.get_barrier_semaphore()
     for step in (-1, 1):
@@ -130,8 +145,8 @@
             pl.semaphore_signal(barrier, inc=1, device_id={"row": z + step}, device_id_type=MESH)
     for copy in loads(0):
         copy.start()
-    mixed_ref[...] = jnp.zeros_like(mixed_ref)
-    d_tokens_ref[...] = jnp.zeros_like(d_tokens_ref)
+    total_ref[...] = jnp.zeros_like(total_ref)
+    depth = down_ref.shape[1]
     pl.semaphore_wait(barrier, jnp.where(near > 0, 2, 1))
 
     @pl.loop(0, units + 2 * middle + 1)
@@ -147,8 +162,7 @@
                     copy.start()
 
             slot, here = lax.rem(t, slots), lax.rem(t, held)
-            for part in range(2):
-                w_in[slot, :, part * wide:(part + 1) * wide] = raw[lax.rem(t, 2), :, part, :]
+            unpack(raw.at[lax.rem(t, 2)], w_in.at[slot], apart)
             partial[here, :, :2 * wide] = dot(rows_ref[...], w_in[slot])
             partial[here, :, 2 * wide:] = dot(cots_ref[...], w_down[slot], OVER_LAST)
 
@@ -216,15 +230,17 @@
                 def _():
                     term_copy(used, side).start()
 
-            out_copy(used).start()
+            for copy in out_copies(used):
+                copy.start()
             slot = lax.rem(used, slots)
-            mixed_ref[...] += dot(terms[used, :, :wide], w_down[slot])
-            d_tokens_ref[...] += dot(terms[used, :, wide:], w_in[slot], OVER_LAST)
+            total_ref[:, :depth] += dot(terms[used, :, :wide], w_down[slot])
+            total_ref[:, depth:] += dot(terms[used, :, wide:], w_in[slot], OVER_LAST)
 
     @pl.loop(0, units)
     def _(u):
         owner = owner_of(u)
-        out_copy(u).wait()
+        for copy in out_copies(u):
+            copy.wait()
 
         @pl.when(owner != z)
         def _():
@@ -259,20 +275,18 @@
     return pl.pallas_call(
         functools.partial(chain_kernel, size, units, wide),
         in_specs=[vmem, vmem, hbm, hbm],
-        out_specs=[vmem, vmem, hbm],
-        out_shape=[
-            jax.ShapeDtypeStruct((count, depth), jnp.float32),
-            jax.ShapeDtypeStruct((count, depth), jnp.float32),
-            jax.ShapeDtypeStruct((count, 3 * width), jnp.bfloat16),
-        ],
+        out_specs=[vmem, hbm, hbm, hbm],
+        out_shape=[jax.ShapeDtypeStruct((count, 2 * depth), jnp.float32)]
+        + 3 * [jax.ShapeDtypeStruct((count, width), jnp.bfloat16)],
         scratch_shapes=[
             pltpu.VMEM((2, depth, 2, wide), jnp.bfloat16),
+            pltpu.VMEM((4, 128, wide), jnp.float32),
             pltpu.VMEM((slots, wide, depth), jnp.bfloat16),
             pltpu.VMEM((slots, depth, 2 * wide), jnp.bfloat16),
             pltpu.VMEM((held, count, 3 * wide), jnp.float32),
             pltpu.VMEM((2, units, count, 3 * wide), sum_type),
             pltpu.VMEM((units, count, 3 * wide), jnp.bfloat16),
-            dma((2, 2)), dma((units,)), dma((2, units)), dma((2, units)), dma((units,)), dma((units,)),
+            dma((2, 2)), dma((units,)), dma((2, units)), dma((2, units)), dma((units,)), dma((3, units)),
         ],
         compiler_params=pltpu.CompilerParams(
             collective_id=collective_id, has_side_effects=True, vmem_limit_bytes=60 * 1024 * 1024
@@ -283,48 +297,6 @@
     )(rows, cotangents, in_weight, down_weight)
 
 
-def weight_kernel(group, wide, rows_ref, cots_ref, terms_ref, d_in_ref, d_down_ref):
-    for g in range(group):
-        columns = slice(g * wide, (g + 1) * wide)
-        base = 3 * g * wide
-        d_down_ref[columns, :] = dot(
-            terms_ref[:, base:base + wide], cots_ref[...], OVER_FIRST
-        ).astype(jnp.bfloat16)
-        both = dot(rows_ref[...], terms_ref[:, base + wide:base + 3 * wide], OVER_FIRST).astype(jnp.bfloat16)
-        for part in range(2):
-            d_in_ref[:, part, columns] = both[:, part * wide:(part + 1) * wide]
-
-
-def weight_gradients(rows, cotangents, terms):
-    count, depth = rows.shape
-    wide = 128
-    width = terms.shape[1] // 3
-    units = width // wide
-    group = 2 if units % 2 == 0 else 1
-    return pl.pallas_call(
-        functools.partial(weight_kernel, group, wide),
-        grid=(units // group,),
-        in_specs=[
-            pl.BlockSpec((count, depth), lambda j: (0, 0)),
-            pl.BlockSpec((count, depth), lambda j: (0, 0)),
-            pl.BlockSpec((count, 3 * group * wide), lambda j: (0, j)),
-        ],
-        out_specs=[
-            pl.BlockSpec((depth, 2, group * wide), lambda j: (0, 0, j)),
-            pl.BlockSpec((group * wide, depth), lambda j: (j, 0)),
-        ],
-        out_shape=[
-            jax.ShapeDtypeStruct((depth, 2, width), jnp.bfloat16),
-            jax.ShapeDtypeStruct((width, depth), jnp.bfloat16),
-        ],
-        cost_estimate=pl.CostEstimate(
-            flops=6 * count * depth * width,
-            bytes_accessed=6 * depth * width + 6 * count * width + 4 * count * depth,
-            transcendentals=0,
-        ),
-    )(rows, cotangents, terms)
-
-
 def per_device(tokens, modality, in_weight, down_weight, d_mixed):
     every = lambda x: lax.all_gather(x, "col", axis=0, tiled=True)
     rows_all = every(tokens)
@@ -339,11 +311,11 @@
         take = lambda x: dot(pick, x).astype(jnp.bfloat16)
         spread = lambda x: dot(pick, x.astype(jnp.bfloat16), OVER_FIRST)
         rows, cotangents = take(rows), take(cotangents)
-        mixed, d_tokens, terms = chain(rows, cotangents, w_in, w_down, 1)
-        d_in, d_down = weight_gradients(rows, cotangents, terms)
-        mixed = exchange(spread(mixed), "col").astype(jnp.bfloat16)
-        d_tokens = exchange(spread(d_tokens), "col").astype(jnp.bfloat16)
-        return (mixed, d_down, d_in, d_tokens)
+        depth = rows.shape[1]
+        total, hidden, d_gate, d_up = chain(rows, cotangents, w_in, w_down, 1)
+        total = exchange(spread(total), "col").astype(jnp.bfloat16)
+        d_down = dot(hidden, cotangents, OVER_FIRST).astype(jnp.bfloat16)
+        return (total[:, :depth], d_down, in_gradient(rows, d_gate, d_up), total[:, depth:])
 
     def whole_form(rows, cotangents, w_in, w_down):
         keep = chosen[:, None].astype(jnp.bfloat16)

time: 411 us -> 314 us (0.76); the launches traced: 403 us -> 314 us
  Pallas kernels: 256 us -> 189 us
  waiting for transfers between devices: 69.4 us -> 54.2 us
  matrix products: 11.6 us -> 24.6 us
  starting transfers between devices: 19 us -> 8.49 us
  loops' own time: 7.55 us -> 0.04 us
    pallas_call x1, Pallas kernels: 81.6 us -> 23.6 us  [in_gradient(): pl.pallas_call(paired_columns, grid=(depth // deep,), in_specs=[pl.BlockS...]
    ppermute x14 -> x7, waiting for transfers between devices: 21.3 us -> 6.69 us  [exchange(): received.append(lax.ppermute(block, axis, moves))]
    dot_general x4, matrix products: 11.6 us -> 24.6 us  [dot(): return lax.dot_general(a, b, dims, preferred_element_type=jnp.float32)]
    ppermute x14 -> x7, starting transfers between devices: 18.9 us -> 8.41 us  [exchange(): received.append(lax.ppermute(block, axis, moves))]
    pallas_call x1, Pallas kernels: 175 us -> 165 us  [chain(): pl.pallas_call(functools.partial(chain_kernel, size, units, wide), in_spe...]
    unnamed x1, loops' own time: 7.55 us -> 0.04 us
  transfers between devices with their start and end apart: 16 -> 9, of which waited for: 7 -> 3; matrix products, arithmetic and copies ran while one was open for 1% -> 4% of each run, Pallas kernels for 20% -> 8%
where the time goes in v1:
time: 314 us
  Pallas kernels  189 us (60%)
  waiting for transfers between devices  54.2 us (17%)
  matrix products  24.6 us (8%)
  between operations  14.7 us (5%)
  blocking collectives  12.8 us (4%)
  starting transfers between devices  8.49 us (3%)
  local copies, waits for them, and re-layouts  6.8 us (2%)
  other arithmetic  3.21 us (1%)
    pallas_call x1, Pallas kernels, chain(): pl.pallas_call(functools.partial(chain_kernel, size, units, wide), in_spe...  165 us
    all_gather x2, waiting for transfers between devices, per_device(): every = lambda x: lax.all_gather(x, 'col', axis=0, tiled=True)  46.2 us
    dot_general x4, matrix products, dot(): return lax.dot_general(a, b, dims, preferred_element_type=jnp.float32)  24.6 us
    pallas_call x1, Pallas kernels, in_gradient(): pl.pallas_call(paired_columns, grid=(depth // deep,), in_specs=[pl.BlockS...  23.6 us
    all_gather x1, blocking collectives, per_device(): chosen = lax.all_gather(modality, 'row', axis=0, tiled=True) == 1  12.8 us
    ppermute x7, starting transfers between devices, exchange(): received.append(lax.ppermute(block, axis, moves))  8.41 us
    ppermute x7, waiting for transfers between devices, exchange(): received.append(lax.ppermute(block, axis, moves))  6.69 us
  transfers between devices with their start and end apart: 9, of which 3 were waited for; matrix products, arithmetic and copies ran while one was open for 4% of the time, Pallas kernels for 8%

profile of v1, /device:TPU:0, one launch (start us, length us, event | category | flops | bytes accessed | tf_op | source)
XLA Modules:
  0.0 313.7 jit_solution(15043503647259890215)
XLA Ops:
  7.2 0.7 all-gather.10.cloned.1.call-update
  7.9 0.7 all-gather.12.cloned.1.call-update
  8.6 12.8 %all-gather = s32[4,1,128]{2,1,0:T(1,128)S(1)} all-gather(s32[1,1,128]{2,1,0:T(1,128)} %bitcast.27), channel_id=1, replica_groups=mesh['row'=4,'col'=8] {'row'}, dimensions={0}, use_global_device_ids=true | all-gather | bytes 2560 | tf_op jit(solution)/shard_map/all_gather | solution.py:304
  22.1 0.6 copy-done.6
  22.7 0.6 slice.30
  23.9 16.5 %all-gather.10.cloned.1.call-done = bf16[512,2048]{1,0:T(8,128)(2,1)} async-done(((bf16[64,2048]{1,0:T(8,128)(2,1)}), bf16[512,2048]{1,0:T(8,128)(2,1)}) %all-gather.10.cloned.1.call-update) | async-done | bytes 2097168 | tf_op jit(solution)/shard_map/all_gather | solution.py:301
  40.4 29.7 %all-gather.12.cloned.1.call-done = bf16[512,2048]{1,0:T(8,128)(2,1)} async-done(((bf16[64,2048]{1,0:T(8,128)(2,1)}), bf16[512,2048]{1,0:T(8,128)(2,1)}) %all-gather.12.cloned.1.call-update) | async-done | bytes 2097168 | tf_op jit(solution)/shard_map/all_gather | solution.py:301
  70.1 236.8 %conditional.2 = (bf16[64,2048]{1,0:T(8,128)(2,1)}, bf16[3584,2048]{1,0:T(8,128)(2,1)}, bf16[2048,2,3584]{2,1,0:T(2,128)(2,1)}, bf16[64,2048]{1,0:T(8,128)(2,1)}) conditional(s32[]{:T(128)} %bitcast.3, (pred[512]{0:T(512)(128)(4,1)S(1)}, bf16[512,2048]{1,0:T(8,128)(2,1)}, bf16[2048,2,3584]{2,1,0:T(2,128)(2,1)}, bf16[3584,2048]{1,0:T(8,128)(2,1)}, ...), branch_computations={%region_2.3_spmd, %region_3.4_spmd} | conditional | flops 67671162880 | bytes 535697504
  70.1 3.6 %convolution_convert_fusion.1.rows_ref = bf16[288,2048]{1,0:T(8,128)(2,1)} fusion(bf16[512,2048]{1,0:T(8,128)(2,1)} %get-tuple-element.34, s32[512]{0:T(512)} %get-tuple-element.33, pred[512]{0:T(512)(128)(4,1)S(1)} %get-tuple-element.32), kind=kOutput, calls=%fused_computation.38 | convolution fusion | flops 604864512 | bytes 3279360 | tf_op jit(solution)/shard_map/cond/branch_1_fun/dot_general | solution.py:16
  73.7 1.8 convolution_convert_fusion.cots_ref
  75.6 165.2 %branch_1_fun.2 = (f32[288,4096]{1,0:T(8,128)}, bf16[288,3584]{1,0:T(8,128)(2,1)}, bf16[288,3584]{1,0:T(8,128)(2,1)}, bf16[288,3584]{1,0:T(8,128)(2,1)}) custom-call(bf16[288,2048]{1,0:T(8,128)(2,1)} %convolution_convert_fusion.1.rows_ref, bf16[288,2048]{1,0:T(8,128)(2,1)} %convolution_convert_fusion.cots_ref, ...), custom_call_target="tpu_custom_call" | custom-call | flops 25367150592 | bytes 44040192 | tf_op jit(solution)/shard_map/cond/branch_1_fun/pallas_call | solution.py:275
  240.8 8.0 %fusion.6 = f32[512,4096]{1,0:T(8,128)} fusion(f32[288,4096]{1,0:T(8,128)} %get-tuple-element.38, s32[512]{0:T(512)S(1)} %copy-done.7, pred[512]{0:T(512)(128)(4,1)S(1)} %get-tuple-element.32), kind=kOutput, calls=%fused_computation.39 | convolution fusion | flops 1209434112 | bytes 13109760 | tf_op jit(solution)/shard_map/cond/branch_1_fun/dot_general | solution.py:16
  248.8 4.6 %dynamic-slice_convert_fusion.26 = (bf16[64,4096]{1,0:T(8,128)(2,1)}, bf16[64,4096]{1,0:T(8,128)(2,1)S(1)}, bf16[64,4096]{1,0:T(8,128)(2,1)S(1)}, bf16[64,4096]{...) fusion(f32[512,4096]{1,0:T(8,128)} %fusion.6, ...), kind=kLoop, calls=%fused_computation.48 | loop fusion | bytes 7340060 | tf_op jit(solution)/shard_map/cond/branch_1_fun/convert_element_type | solution.py:26
  253.4 2.6 collective-permute-start.26
  256.0 0.5 collective-permute-start.25
  256.5 0.6 collective-permute-start.24
  257.1 0.9 collective-permute-start.23
  258.0 11.1 %fusion.23 = bf16[3584,2048]{1,0:T(8,128)(2,1)} fusion(bf16[288,3584]{1,0:T(8,128)(2,1)S(1)} %copy-done.11, bf16[288,2048]{1,0:T(8,128)(2,1)S(1)} %copy-done.10), kind=kOutput, calls=%fused_computation.66 | convolution fusion | flops 4227858432 | bytes 17924096 | tf_op jit(solution)/shard_map/cond/branch_1_fun/dot_general | solution.py:16
  269.1 1.5 collective-permute-start.22
  270.6 2.3 collective-permute-start.21
  272.9 23.6 %branch_1_fun.3 = bf16[2048,2,3584]{2,1,0:T(2,128)(2,1)} custom-call(bf16[288,2048]{1,0:T(8,128)(2,1)} %convolution_convert_fusion.1.rows_ref, bf16[288,3584]{1,0:T(8,128)(2,1)} %get-tuple-element.40.gate_ref, bf16[288,3584]{1,0:T(8,128)(2,1)} %get-tuple-element.41.up_ref), custom_call_target="tpu_custom_call" | custom-call | flops 8455716864 | bytes 35848192 | tf_op jit(solution)/shard_map/cond/branch_1_fun/pallas_call | solution.py:44
  296.6 6.7 %collective-permute-done.22 = bf16[64,4096]{1,0:T(8,128)(2,1)} collective-permute-done((bf16[64,4096]{1,0:T(8,128)(2,1)S(1)}, bf16[64,4096]{1,0:T(8,128)(2,1)}, u32[]{:S(2)}, u32[]{:S(2)}) %collective-permute-start.22) | collective-permute-done | bytes 524320 | tf_op jit(solution)/shard_map/cond/branch_1_fun/ppermute | solution.py:28
  303.3 2.8 add_convert_fusion.2
  306.0 0.8 fusion.19
  (25 shorter events, 0.7 us)
Async XLA Ops:
  7.2 33.2 %all-gather.10.cloned.1.call-start = ((), (), s32[]{:S(2)}) async-start(), calls=%async_computation.2 | async-start | bytes 2359296 | tf_op jit(solution)/shard_map/all_gather | solution.py:301
  7.9 62.2 %all-gather.12.cloned.1.call-start = ((), (), s32[]{:S(2)}) async-start(), calls=%async_computation.3 | async-start | bytes 2359296 | tf_op jit(solution)/shard_map/all_gather | solution.py:301
  22.1 0.6 copy-start.6
  70.1 3.6 %copy-start.7 = (s32[512]{0:T(512)S(1)}, s32[512]{0:T(512)}, u32[]{:S(2)}) copy-start(s32[512]{0:T(512)} %get-tuple-element.33) | copy-start | bytes 6148 | tf_op jit(solution)/shard_map/conditional
  70.1 3.6 %copy-start.9 = (bf16[512,2048]{1,0:T(8,128)(2,1)S(1)}, bf16[512,2048]{1,0:T(8,128)(2,1)}, u32[]{:S(2)}) copy-start(bf16[512,2048]{1,0:T(8,128)(2,1)} %get-tuple-element.35) | copy-start | bytes 6291460 | tf_op jit(solution)/shard_map/conditional
  248.8 9.2 %copy-start.10 = (bf16[288,2048]{1,0:T(8,128)(2,1)S(1)}, bf16[288,2048]{1,0:T(8,128)(2,1)}, u32[]{:S(2)}) copy-start(bf16[288,2048]{1,0:T(8,128)(2,1)} %convolution_convert_fusion.cots_ref) | copy-start | bytes 3538948 | tf_op jit(solution)/shard_map/conditional
  248.8 9.2 %copy-start.11 = (bf16[288,3584]{1,0:T(8,128)(2,1)S(1)}, bf16[288,3584]{1,0:T(8,128)(2,1)}, u32[]{:S(2)}) copy-start(bf16[288,3584]{1,0:T(8,128)(2,1)} %get-tuple-element.39) | copy-start | bytes 6193156 | tf_op jit(solution)/shard_map/conditional
  253.4 15.8 %collective-permute-start.20 = (bf16[64,4096]{1,0:T(8,128)(2,1)}, bf16[64,4096]{1,0:T(8,128)(2,1)}, u32[]{:S(2)}, u32[]{:S(2)}) collective-permute-start(bf16[64,4096]{1,0:T(8,128)(2,1)} %get-tuple-element.79), channel_id=1, source_target_pairs={{0,1},{1,2},{2,3},{3,4},{4,5},{5,6},{6,7},{7,0},{8,9},{9,10},{10,1... | collective-permute-start | bytes 1572872 | tf_op jit(solution)/shard_map/cond/branch_1_fun/ppermute | solution.py:28
  253.4 17.2 %collective-permute-start.26 = (bf16[64,4096]{1,0:T(8,128)(2,1)S(1)}, bf16[64,4096]{1,0:T(8,128)(2,1)}, u32[]{:S(2)}, u32[]{:S(2)}) collective-permute-start(bf16[64,4096]{1,0:T(8,128)(2,1)S(1)} %get-tuple-element.80), channel_id=1, source_target_pairs={{0,7},{1,0},{2,1},{3,2},{4,3},{5,4},{6,5},{7,6},{8,15},{9,8},{10,9... | collective-permute-start | bytes 1572872 | tf_op jit(solution)/shard_map/cond/branch_1_fun/ppermute | solution.py:28
  256.0 40.5 %collective-permute-start.25 = (bf16[64,4096]{1,0:T(8,128)(2,1)S(1)}, bf16[64,4096]{1,0:T(8,128)(2,1)}, u32[]{:S(2)}, u32[]{:S(2)}) collective-permute-start(bf16[64,4096]{1,0:T(8,128)(2,1)S(1)} %get-tuple-element.81), channel_id=1, source_target_pairs={{0,6},{1,7},{2,0},{3,1},{4,2},{5,3},{6,4},{7,5},{8,14},{9,15},{10,... | collective-permute-start | bytes 1572872 | tf_op jit(solution)/shard_map/cond/branch_1_fun/ppermute | solution.py:28
  256.5 40.0 %collective-permute-start.24 = (bf16[64,4096]{1,0:T(8,128)(2,1)S(1)}, bf16[64,4096]{1,0:T(8,128)(2,1)}, u32[]{:S(2)}, u32[]{:S(2)}) collective-permute-start(bf16[64,4096]{1,0:T(8,128)(2,1)S(1)} %get-tuple-element.82), channel_id=1, source_target_pairs={{0,5},{1,6},{2,7},{3,0},{4,1},{5,2},{6,3},{7,4},{8,13},{9,14},{10,... | collective-permute-start | bytes 1572872 | tf_op jit(solution)/shard_map/cond/branch_1_fun/ppermute | solution.py:28
  257.1 39.5 %collective-permute-start.23 = (bf16[64,4096]{1,0:T(8,128)(2,1)S(1)}, bf16[64,4096]{1,0:T(8,128)(2,1)}, u32[]{:S(2)}, u32[]{:S(2)}) collective-permute-start(bf16[64,4096]{1,0:T(8,128)(2,1)S(1)} %get-tuple-element.83), channel_id=1, source_target_pairs={{0,4},{1,5},{2,6},{3,7},{4,0},{5,1},{6,2},{7,3},{8,12},{9,13},{10,... | collective-permute-start | bytes 1572872 | tf_op jit(solution)/shard_map/cond/branch_1_fun/ppermute | solution.py:28
  269.1 34.1 %collective-permute-start.22 = (bf16[64,4096]{1,0:T(8,128)(2,1)S(1)}, bf16[64,4096]{1,0:T(8,128)(2,1)}, u32[]{:S(2)}, u32[]{:S(2)}) collective-permute-start(bf16[64,4096]{1,0:T(8,128)(2,1)S(1)} %get-tuple-element.84), channel_id=1, source_target_pairs={{0,3},{1,4},{2,5},{3,6},{4,7},{5,0},{6,1},{7,2},{8,11},{9,12},{10,... | collective-permute-start | bytes 1572872 | tf_op jit(solution)/shard_map/cond/branch_1_fun/ppermute | solution.py:28
  270.6 32.7 %collective-permute-start.21 = (bf16[64,4096]{1,0:T(8,128)(2,1)S(1)}, bf16[64,4096]{1,0:T(8,128)(2,1)S(1)}, u32[]{:S(2)}, u32[]{:S(2)}) collective-permute-start(bf16[64,4096]{1,0:T(8,128)(2,1)S(1)} %get-tuple-element.85), channel_id=1, source_target_pairs={{0,2},{1,3},{2,4},{3,5},{4,6},{5,7},{6,0},{7,1},{8,10},{9,11},{10,... | collective-permute-start | bytes 1572872 | tf_op jit(solution)/shard_map/cond/branch_1_fun/ppermute | solution.py:28
Sparse Core Ops, SparseCore 0:
  9.9 30.5 all-gather.9
  42.3 27.7 all-gather.11

commit v2 on v1

--- a/solution.py
+++ b/solution.py
@@ -1,4 +1,5 @@
 import functools
+import math
 
 import jax
 import jax.numpy as jnp
@@ -32,20 +33,32 @@
     return total
 
 
+def gather(block, axis):
+    count = lax.axis_size(axis)
+    me = lax.axis_index(axis)
+    out = jnp.zeros((count,) + block.shape, block.dtype)
+    out = lax.dynamic_update_index_in_dim(out, block, me, 0)
+    for shift in range(1, count):
+        moves = [(i, (i + shift) % count) for i in range(count)]
+        arrived = lax.ppermute(block, axis, moves)
+        out = lax.dynamic_update_index_in_dim(out, arrived, lax.rem(me + count - shift, count), 0)
+    return out.reshape((count * block.shape[0],) + block.shape[1:])
+
+
 def paired_columns(rows_ref, gate_ref, up_ref, out_ref):
     for part, side_ref in enumerate((gate_ref, up_ref)):
         out_ref[:, part, :] = dot(rows_ref[...], side_ref[...], OVER_FIRST).astype(jnp.bfloat16)
 
 
-def in_gradient(rows, d_gate, d_up):
-    count, depth = rows.shape
+def in_gradient(packed, d_gate, d_up):
+    _, count, depth = packed.shape
     width = d_gate.shape[1]
     deep = depth // 8
     return pl.pallas_call(
         paired_columns,
         grid=(depth // deep,),
         in_specs=[
-            pl.BlockSpec((count, deep), lambda i: (0, i)),
+            pl.BlockSpec((None, count, deep), lambda i: (0, 0, i)),
             pl.BlockSpec((count, width), lambda i: (0, 0)),
             pl.BlockSpec((count, width), lambda i: (0, 0)),
         ],
@@ -56,7 +69,7 @@
             bytes_accessed=4 * (depth * width + count * width + count * depth),
             transcendentals=0,
         ),
-    )(rows, d_gate, d_up)
+    )(packed, d_gate, d_up)
 
 
 def swiglu_terms(gate, up, d_hidden):
@@ -73,12 +86,161 @@
     projected = exchange(dot(rows, flat_in), "row")
     hidden, d_gate, d_up = swiglu_terms(projected[:, :width], projected[:, width:], d_hidden)
     d_local = jnp.concatenate([d_gate, d_up], 1).astype(jnp.bfloat16)
-    hidden_all = lax.all_gather(hidden.astype(jnp.bfloat16), "row", axis=0, tiled=True)
-    d_projected = lax.all_gather(d_local, "row", axis=0, tiled=True)
+    hidden_all = gather(hidden.astype(jnp.bfloat16), "row")
+    d_projected = gather(d_local, "row")
     mixed = exchange(dot(hidden_all, down_weight), "col").astype(jnp.bfloat16)
     d_down = dot(hidden_all, cotangents, OVER_FIRST).astype(jnp.bfloat16)
     d_tokens = exchange(dot(d_projected, flat_in, OVER_LAST), "col").astype(jnp.bfloat16)
-    return (mixed, d_down, in_gradient(rows, d_projected[:, :width], d_projected[:, width:]), d_tokens)
+    return (mixed, d_down, in_gradient(rows[None], d_projected[:, :width], d_projected[:, width:]), d_tokens)
+
+
+def gather_kernel(
+    size, side, tokens_ref, modality_ref, d_mixed_ref, packed_ref, pick_ref, count_ref,
+    whole, chosen, local_sem, mate_send, mate_recv, send, recv, row_send, row_recv, hand_send, hand_recv,
+):
+    z, column = lax.axis_index("row"), lax.axis_index("col")
+    core, chip = lax.rem(column, 2), column // 2
+    y, x = chip // side, lax.rem(chip, side)
+    rows = tokens_ref.shape[0]
+    chips = side * side
+
+    def at(part):
+        return whole.at[pl.ds(pl.multiple_of(part * rows, rows), rows), :]
+
+    def remote(src, dst, send_sem, recv_sem, where):
+        return pltpu.make_async_remote_copy(
+            src_ref=src, dst_ref=dst, send_sem=send_sem, recv_sem=recv_sem, device_id=where, device_id_type=MESH
+        )
+
+    def chip_of(dy, dx):
+        return lax.rem(y + dy, side) * side + lax.rem(x + dx, side)
+
+    mate = {"col": chip * 2 + 1 - core}
+    others = [(dy, dx) for dy in range(side) for dx in range(side) if dy or dx]
+    if side == 2:
+        straight = [(0, 1), (1, 0)]
+    else:
+        straight = others
+
+    def block_copy(k, source, half, dy, dx):
+        part = source * 2 + half
+        return remote(at(part), at(part), send.at[k], recv.at[part], {"col": chip_of(dy, dx) * 2 + core})
+
+    def arrival(part):
+        return remote(at(part), at(part), send.at[0], recv.at[part], mate)
+
+    barrier = pltpu.get_barrier_semaphore()
+    pl.semaphore_signal(barrier, inc=1, device_id=mate, device_id_type=MESH)
+    for dy, dx in straight:
+        pl.semaphore_signal(
+            barrier, inc=1, device_id={"col": chip_of(dy, dx) * 2 + core}, device_id_type=MESH
+        )
+    for step in range(1, size):
+        pl.semaphore_signal(barrier, inc=1, device_id={"row": lax.rem(z + step, size)}, device_id_type=MESH)
+    mine = chip * 2 + core
+    for k, (kept, given) in enumerate(((tokens_ref, d_mixed_ref), (d_mixed_ref, tokens_ref))):
+        @pl.when(core == k)
+        def _():
+            pltpu.make_async_copy(kept, at(mine), local_sem.at[0]).start()
+
+    pltpu.make_async_copy(modality_ref, chosen.at[z], local_sem.at[1]).start()
+    pl.semaphore_wait(barrier, len(straight) + size)
+
+    def mate_copy(given):
+        return remote(given, at(mine), mate_send, mate_recv, mate)
+
+    for k, given in enumerate((d_mixed_ref, tokens_ref)):
+        @pl.when(core == k)
+        def _():
+            mate_copy(given).start()
+
+    row_copies = [
+        remote(
+            modality_ref, chosen.at[z], row_send.at[step - 1], row_recv.at[step - 1],
+            {"row": lax.rem(z + step, size)},
+        )
+        for step in range(1, size)
+    ]
+    for copy in row_copies:
+        copy.start()
+    pltpu.make_async_copy(tokens_ref, at(mine), local_sem.at[0]).wait()
+    first = [block_copy(k, chip, core, dy, dx) for k, (dy, dx) in enumerate(straight)]
+    for copy in first:
+        copy.start()
+    mate_copy(tokens_ref).wait_recv()
+    base = len(straight)
+    second = [block_copy(base + k, chip, 1 - core, dy, dx) for k, (dy, dx) in enumerate(straight)]
+    for copy in second:
+        copy.start()
+    relays = []
+    if side == 2:
+        arrival(chip_of(0, 1) * 2).wait_recv()
+        relays.append(block_copy(2 * base, chip_of(0, 1), 0, 1, 0))
+        relays[-1].start()
+        arrival(chip_of(1, 0) * 2 + 1).wait_recv()
+        relays.append(block_copy(2 * base + 1, chip_of(1, 0), 1, 0, 1))
+        relays[-1].start()
+
+    pltpu.make_async_copy(modality_ref, chosen.at[z], local_sem.at[1]).wait()
+    for copy in row_copies:
+        copy.wait_recv()
+    total = whole.shape[0]
+    picked = jnp.concatenate([chosen[k] for k in range(size)], axis=1) == 1
+    ones = jnp.broadcast_to(picked.astype(jnp.float32), (8, total))
+    up_to = lax.broadcasted_iota(jnp.int32, (total, total), 0) <= lax.broadcasted_iota(
+        jnp.int32, (total, total), 1
+    )
+    running = dot(ones.astype(jnp.bfloat16), up_to.astype(jnp.float32).astype(jnp.bfloat16))
+    place = jnp.where(ones > 0.5, running, 0.0)[:1].astype(jnp.int32) - 1
+    slot = lax.broadcasted_iota(jnp.int32, pick_ref.shape, 0)
+    pick_ref[...] = (slot == place).astype(jnp.float32).astype(jnp.bfloat16)
+    count_ref[...] = jnp.broadcast_to(jnp.sum(ones[:1], axis=1, keepdims=True), count_ref.shape)
+
+    if side == 2:
+        rest = [
+            (chip_of(0, 1), 1), (chip_of(1, 0), 0), (chip_of(1, 1), 0), (chip_of(1, 1), 1),
+        ]
+    else:
+        rest = [(chip_of(dy, dx), half) for dy, dx in others for half in range(2)]
+    for source, half in rest:
+        arrival(source * 2 + half).wait_recv()
+    packed_ref[core] = dot(pick_ref[...], whole[...]).astype(jnp.bfloat16)
+    hand = remote(packed_ref.at[core], packed_ref.at[core], hand_send, hand_recv, mate)
+    hand.start()
+    for copy in first + second + relays + row_copies:
+        copy.wait_send()
+    mate_copy(tokens_ref).wait_send()
+    hand.wait_send()
+    remote(packed_ref.at[1 - core], packed_ref.at[1 - core], hand_send, hand_recv, mate).wait_recv()
+
+
+def gather_packed(tokens, modality, d_mixed, packed, collective_id):
+    size, columns = lax.axis_size("row"), lax.axis_size("col")
+    side = math.isqrt(columns // 2)
+    rows, depth = tokens.shape
+    total = rows * columns
+    sends = 6 if side == 2 else 2 * (side * side - 1)
+    vmem = pl.BlockSpec(memory_space=pltpu.VMEM)
+    dma = pltpu.SemaphoreType.DMA
+    return pl.pallas_call(
+        functools.partial(gather_kernel, size, side),
+        in_specs=[vmem] * 3,
+        out_specs=[vmem] * 3,
+        out_shape=[
+            jax.ShapeDtypeStruct((2, packed, depth), jnp.bfloat16),
+            jax.ShapeDtypeStruct((packed, total), jnp.bfloat16),
+            jax.ShapeDtypeStruct((8, 128), jnp.float32),
+        ],
+        scratch_shapes=[
+            pltpu.VMEM((total, depth), jnp.bfloat16),
+            pltpu.VMEM((size, 1, total // size), jnp.int32),
+            dma((2,)), dma, dma, dma((sends,)), dma((columns,)), dma((size - 1,)), dma((size - 1,)), dma, dma,
+        ],
+        compiler_params=pltpu.CompilerParams(collective_id=collective_id, has_side_effects=True),
+        cost_estimate=pl.CostEstimate(
+            flops=2 * packed * total * depth, bytes_accessed=4 * total * depth, transcendentals=0
+        ),
+    )(tokens, modality.reshape(1, -1), d_mixed)
 
 
 def unpack(pairs_ref, columns_ref, apart):
@@ -93,7 +255,7 @@
 
 
 def chain_kernel(
-    size, units, wide, rows_ref, cots_ref, in_ref, down_ref, total_ref, hidden_ref, d_gate_ref, d_up_ref,
+    size, units, wide, packed_ref, in_ref, down_ref, total_ref, hidden_ref, d_gate_ref, d_up_ref,
     raw, apart, w_down, w_in, partial, sums, terms,
     load_sem, sum_send, sum_recv, term_send, term_recv, out_sem,
 ):
@@ -163,8 +325,8 @@
 
             slot, here = lax.rem(t, slots), lax.rem(t, held)
             unpack(raw.at[lax.rem(t, 2)], w_in.at[slot], apart)
-            partial[here, :, :2 * wide] = dot(rows_ref[...], w_in[slot])
-            partial[here, :, 2 * wide:] = dot(cots_ref[...], w_down[slot], OVER_LAST)
+            partial[here, :, :2 * wide] = dot(packed_ref[0], w_in[slot])
+            partial[here, :, 2 * wide:] = dot(packed_ref[1], w_down[slot], OVER_LAST)
 
         relayed = t - near
 
@@ -261,9 +423,9 @@
                 term_copy(u, 1).wait_send()
 
 
-def chain(rows, cotangents, in_weight, down_weight, collective_id):
+def chain(packed, in_weight, down_weight, collective_id):
     size = lax.axis_size("row")
-    count, depth = rows.shape
+    _, count, depth = packed.shape
     width = down_weight.shape[0]
     wide = 128
     units = width // wide
@@ -274,7 +436,7 @@
     dma = pltpu.SemaphoreType.DMA
     return pl.pallas_call(
         functools.partial(chain_kernel, size, units, wide),
-        in_specs=[vmem, vmem, hbm, hbm],
+        in_specs=[vmem, hbm, hbm],
         out_specs=[vmem, hbm, hbm, hbm],
         out_shape=[jax.ShapeDtypeStruct((count, 2 * depth), jnp.float32)]
         + 3 * [jax.ShapeDtypeStruct((count, width), jnp.bfloat16)],
@@ -294,35 +456,29 @@
         cost_estimate=pl.CostEstimate(
             flops=12 * count * depth * width, bytes_accessed=6 * depth * width, transcendentals=count * width
         ),
-    )(rows, cotangents, in_weight, down_weight)
+    )(packed, in_weight, down_weight)
 
 
 def per_device(tokens, modality, in_weight, down_weight, d_mixed):
-    every = lambda x: lax.all_gather(x, "col", axis=0, tiled=True)
-    rows_all = every(tokens)
-    cots_all = every(d_mixed)
-    chosen = lax.all_gather(modality, "row", axis=0, tiled=True) == 1
-    total = chosen.shape[0]
-    place = jnp.cumsum(chosen.astype(jnp.int32)) - 1
-    packed = total * 9 // 16
-
-    def packed_form(rows, cotangents, w_in, w_down):
-        pick = (chosen[None, :] & (place[None, :] == jnp.arange(packed)[:, None])).astype(jnp.bfloat16)
-        take = lambda x: dot(pick, x).astype(jnp.bfloat16)
-        spread = lambda x: dot(pick, x.astype(jnp.bfloat16), OVER_FIRST)
-        rows, cotangents = take(rows), take(cotangents)
-        depth = rows.shape[1]
-        total, hidden, d_gate, d_up = chain(rows, cotangents, w_in, w_down, 1)
-        total = exchange(spread(total), "col").astype(jnp.bfloat16)
-        d_down = dot(hidden, cotangents, OVER_FIRST).astype(jnp.bfloat16)
-        return (total[:, :depth], d_down, in_gradient(rows, d_gate, d_up), total[:, depth:])
-
-    def whole_form(rows, cotangents, w_in, w_down):
-        keep = chosen[:, None].astype(jnp.bfloat16)
-        return block_terms(rows * keep, cotangents * keep, w_in, w_down)
+    total = tokens.shape[0] * lax.axis_size("col")
+    depth = tokens.shape[1]
+    room = total * 9 // 16
+    packed, pick, count = gather_packed(tokens, modality, d_mixed, room, 2)
+
+    def packed_form(packed, pick, tokens, modality, d_mixed, w_in, w_down):
+        total, hidden, d_gate, d_up = chain(packed, w_in, w_down, 1)
+        total = exchange(dot(pick, total.astype(jnp.bfloat16), OVER_FIRST), "col").astype(jnp.bfloat16)
+        d_down = dot(hidden, packed[1], OVER_FIRST).astype(jnp.bfloat16)
+        return (total[:, :depth], d_down, in_gradient(packed, d_gate, d_up), total[:, depth:])
+
+    def whole_form(packed, pick, tokens, modality, d_mixed, w_in, w_down):
+        keep = (gather(modality, "row") == 1)[:, None].astype(jnp.bfloat16)
+        both = gather(jnp.concatenate([tokens, d_mixed], 1), "col") * keep
+        return block_terms(both[:, :depth], both[:, depth:], w_in, w_down)
 
     return lax.cond(
-        place[-1] < packed, packed_form, whole_form, rows_all, cots_all, in_weight, down_weight
+        count[0, 0] <= room, packed_form, whole_form,
+        packed, pick, tokens, modality, d_mixed, in_weight, down_weight,
     )
 
 

time: 314 us -> 261 us (0.83)
  waiting for transfers between devices: 54.2 us -> 6.23 us
  Pallas kernels: 189 us -> 218 us
  between operations: 14.7 us -> 1.29 us
  blocking collectives: 12.8 us -> 0 us
  matrix products: 24.6 us -> 15.8 us
    all_gather x2 -> x0, waiting for transfers between devices: 46.2 us -> none  [per_device(): every = lambda x: lax.all_gather(x, 'col', axis=0, tiled=True)]
    pallas_call x0 -> x1, Pallas kernels: none -> 30.1 us  [gather_packed(): pl.pallas_call(functools.partial(gather_kernel, size, side), in_specs=[vm...]
    all_gather x1 -> x0, blocking collectives: 12.8 us -> none  [per_device(): chosen = lax.all_gather(modality, 'row', axis=0, tiled=True) == 1]
    dot_general x4 -> x2, matrix products: 24.6 us -> 15.8 us  [dot(): return lax.dot_general(a, b, dims, preferred_element_type=jnp.float32)]
    another operation x9 -> x6, local copies, waits for them, and re-layouts: 0.13 us -> 3.35 us
  transfers between devices with their start and end apart: 9 -> 7, of which waited for: 3 -> 1; matrix products, arithmetic and copies ran while one was open for 4% -> 4% of each run, Pallas kernels for 8% -> 9%
where the time goes in v2:
time: 261 us; the launch traced here: 260 us
  Pallas kernels  218 us (84%)
  matrix products  15.8 us (6%)
  starting transfers between devices  8.55 us (3%)
  local copies, waits for them, and re-layouts  6.97 us (3%)
  waiting for transfers between devices  6.23 us (2%)
  other arithmetic  2.92 us (1%)
    pallas_call x1, Pallas kernels, chain(): pl.pallas_call(functools.partial(chain_kernel, size, units, wide), in_spe...  164 us
    pallas_call x1, Pallas kernels, gather_packed(): pl.pallas_call(functools.partial(gather_kernel, size, side), in_specs=[vm...  30.1 us
    pallas_call x1, Pallas kernels, in_gradient(): pl.pallas_call(paired_columns, grid=(depth // deep,), in_specs=[pl.BlockS...  23.6 us
    dot_general x2, matrix products, dot(): return lax.dot_general(a, b, dims, preferred_element_type=jnp.float32)  15.8 us
    ppermute x7, starting transfers between devices, exchange(): received.append(lax.ppermute(block, axis, moves))  8.55 us
    ppermute x7, waiting for transfers between devices, exchange(): received.append(lax.ppermute(block, axis, moves))  6.23 us
  transfers between devices with their start and end apart: 7, of which 1 were waited for; matrix products, arithmetic and copies ran while one was open for 4% of the time, Pallas kernels for 9%

profile of v2, /device:TPU:0, one launch (start us, length us, event | category | flops | bytes accessed | tf_op | source)
XLA Modules:
  0.0 260.1 jit_solution(9341410279751793226)
XLA Ops:
  0.6 30.1 %shard_map.84 = (bf16[2,288,2048]{2,1,0:T(8,128)(2,1)}, bf16[288,512]{1,0:T(8,128)(2,1)S(1)}, f32[8,128]{1,0:T(8,128)}) custom-call(bf16[64,2048]{1,0:T(8,128)(2,1)} %tokens_ref.1, s32[1,128]{1,0:T(1,128)} %bitcast.99, bf16[64,2048]{1,0:T(8,128)(2,1)} %d_mixed_ref.1), custom_call_target="tpu_custom_call" | custom-call | flops 603979776 | bytes 4194304 | tf_op jit(solution)/shard_map/pallas_call | solution.py:225
  30.8 1.2 slice.30
  32.6 227.4 %conditional.2 = (bf16[64,2048]{1,0:T(8,128)(2,1)}, bf16[3584,2048]{1,0:T(8,128)(2,1)}, bf16[2048,2,3584]{2,1,0:T(2,128)(2,1)}, bf16[64,2048]{1,0:T(8,128)(2,1)}) conditional(s32[]{:T(128)} %bitcast.36, (bf16[64,2048]{1,0:T(8,128)(2,1)}, bf16[64,2048]{1,0:T(8,128)(2,1)}, s32[128]{0:T(128)}, bf16[2048,2,3584]{2,1,0:T(2,128)(2,1)}, ...), branch_computations={%region_0.1_spmd, %region_1.2_spmd} | conditional | flops 67675619328 | bytes 530732640
  32.9 164.2 %branch_1_fun.2 = (f32[288,4096]{1,0:T(8,128)}, bf16[288,3584]{1,0:T(8,128)(2,1)}, bf16[288,3584]{1,0:T(8,128)(2,1)}, bf16[288,3584]{1,0:T(8,128)(2,1)}) custom-call(bf16[2,288,2048]{2,1,0:T(8,128)(2,1)} %get-tuple-element.28.packed_ref.rows_ref, bf16[2048,2,3584]{2,1,0:T(2,128)(2,1)} %get-tuple-element.29.in_ref, bf16[3584,2048]{1,0:T(8,128)(2,1)} %get-tuple-element.30.down_ref), custom_call_target="tpu_custom_call" | custom-call | flops 25367150592 | bytes 44040192 | tf_op jit(solution)/shard_map/cond/branch_1_fun/pallas_call | solution.py:437
  197.1 4.7 %fusion.7 = f32[4096,512]{0,1:T(8,128)S(1)} fusion(bf16[288,512]{1,0:T(8,128)(2,1)S(1)} %get-tuple-element.32, f32[288,4096]{1,0:T(8,128)} %get-tuple-element.31), kind=kOutput, calls=%fused_computation.58 | convolution fusion | flops 1209139200 | bytes 13402112 | tf_op jit(solution)/shard_map/cond/branch_1_fun/dot_general | solution.py:17
  201.8 3.3 %copy-done = f32[4096,512]{0,1:T(8,128)} copy-done((f32[4096,512]{0,1:T(8,128)}, f32[4096,512]{0,1:T(8,128)S(1)}, u32[]{:S(2)}) %copy-start) | copy-done | bytes 8388632 | tf_op jit(solution)/shard_map/conditional
  205.2 1.6 fusion.19
  206.8 0.0 collective-permute-start.36
  206.8 2.6 %collective-permute-start.42 = (bf16[64,4096]{1,0:T(8,128)(2,1)}, bf16[64,4096]{1,0:T(8,128)(2,1)}, u32[]{:S(2)}, u32[]{:S(2)}) collective-permute-start(bf16[64,4096]{1,0:T(8,128)(2,1)} %get-tuple-element.57), channel_id=1, source_target_pairs={{0,7},{1,0},{2,1},{3,2},{4,3},{5,4},{6,5},{7,6},{8,15},{9,8},{10,9... | collective-permute-start | bytes 1572872 | tf_op jit(solution)/shard_map/cond/branch_1_fun/ppermute | solution.py:29
  209.4 1.3 collective-permute-start.41
  210.7 0.0 collective-permute-start.40
  210.7 0.8 collective-permute-start.39
  211.5 11.1 %fusion.9 = bf16[3584,2048]{1,0:T(8,128)(2,1)} fusion(bf16[288,3584]{1,0:T(8,128)(2,1)S(1)} %copy-done.6, bf16[2,288,2048]{2,1,0:T(8,128)(2,1)S(1)} %copy-done.2), kind=kOutput, calls=%fused_computation.60 | convolution fusion | flops 4227858432 | bytes 17924096 | tf_op jit(solution)/shard_map/cond/branch_1_fun/dot_general | solution.py:17
  222.6 0.0 collective-permute-done.36
  222.6 1.5 collective-permute-start.38
  224.1 0.0 collective-permute-done.42
  224.1 2.4 collective-permute-start.37
  226.4 23.6 %branch_1_fun.3 = bf16[2048,2,3584]{2,1,0:T(2,128)(2,1)} custom-call(bf16[2,288,2048]{2,1,0:T(8,128)(2,1)S(1)} %copy-done.2, bf16[288,3584]{1,0:T(8,128)(2,1)} %get-tuple-element.34.gate_ref, bf16[288,3584]{1,0:T(8,128)(2,1)} %get-tuple-element.35.up_ref), custom_call_target="tpu_custom_call" | custom-call | flops 8455716864 | bytes 35848192 | tf_op jit(solution)/shard_map/cond/branch_1_fun/pallas_call | solution.py:57
  250.1 0.0 collective-permute-done.41
  250.1 0.0 collective-permute-done.40
  250.1 0.0 collective-permute-done.39
  250.1 6.2 %collective-permute-done.38 = bf16[64,4096]{1,0:T(8,128)(2,1)} collective-permute-done((bf16[64,4096]{1,0:T(8,128)(2,1)S(1)}, bf16[64,4096]{1,0:T(8,128)(2,1)}, u32[]{:S(2)}, u32[]{:S(2)}) %collective-permute-start.38) | collective-permute-done | bytes 524320 | tf_op jit(solution)/shard_map/cond/branch_1_fun/ppermute | solution.py:29
  256.3 2.9 %fusion.18 = bf16[64,4096]{1,0:T(8,128)(2,1)S(1)} fusion(bf16[64,4096]{1,0:T(8,128)(2,1)} %collective-permute-done.42, bf16[64,4096]{1,0:T(8,128)(2,1)} %collective-permute-done.41, bf16[64,4096]{1,0:T(8,128)(2,1)} %collective-permute-done.40, bf16[64,4096]{1,0:T(8,128)(2,1)} %collective-permute-done.39, bf16[64,4096]{1,0:T(8,128)(2,1)} %collective-permute-done.38, ...), kind=kLoop, calls=%fused_computation.70 | loop fusion | flops 3932160 | bytes 5242884 | tf_op jit(solution)/shard_map/cond/branch_1_fun/convert_element_type | solution.py:470
  259.2 0.8 fusion.26
  (6 shorter events, 0.0 us)
Async XLA Ops:
  201.8 3.3 %copy-start = (f32[4096,512]{0,1:T(8,128)}, f32[4096,512]{0,1:T(8,128)S(1)}, u32[]{:S(2)}) copy-start(f32[4096,512]{0,1:T(8,128)S(1)} %fusion.7) | copy-start | bytes 25165828 | tf_op jit(solution)/shard_map/conditional
  205.2 6.3 %copy-start.2 = (bf16[2,288,2048]{2,1,0:T(8,128)(2,1)S(1)}, bf16[2,288,2048]{2,1,0:T(8,128)(2,1)}, u32[]{:S(2)}) copy-start(bf16[2,288,2048]{2,1,0:T(8,128)(2,1)} %get-tuple-element.28.packed_ref.rows_ref) | copy-start | bytes 7077892 | tf_op jit(solution)/shard_map/conditional
  205.2 6.3 %copy-start.6 = (bf16[288,3584]{1,0:T(8,128)(2,1)S(1)}, bf16[288,3584]{1,0:T(8,128)(2,1)}, u32[]{:S(2)}) copy-start(bf16[288,3584]{1,0:T(8,128)(2,1)} %get-tuple-element.33) | copy-start | bytes 6193156 | tf_op jit(solution)/shard_map/conditional
  206.8 15.8 %collective-permute-start.36 = (bf16[64,4096]{1,0:T(8,128)(2,1)}, bf16[64,4096]{1,0:T(8,128)(2,1)}, u32[]{:S(2)}, u32[]{:S(2)}) collective-permute-start(bf16[64,4096]{1,0:T(8,128)(2,1)} %get-tuple-element.56), channel_id=1, source_target_pairs={{0,1},{1,2},{2,3},{3,4},{4,5},{5,6},{6,7},{7,0},{8,9},{9,10},{10,1... | collective-permute-start | bytes 1572872 | tf_op jit(solution)/shard_map/cond/branch_1_fun/ppermute | solution.py:29
  206.8 17.3 %collective-permute-start.42 = (bf16[64,4096]{1,0:T(8,128)(2,1)}, bf16[64,4096]{1,0:T(8,128)(2,1)}, u32[]{:S(2)}, u32[]{:S(2)}) collective-permute-start(bf16[64,4096]{1,0:T(8,128)(2,1)} %get-tuple-element.57), channel_id=1, source_target_pairs={{0,7},{1,0},{2,1},{3,2},{4,3},{5,4},{6,5},{7,6},{8,15},{9,8},{10,9... | collective-permute-start | bytes 1572872 | tf_op jit(solution)/shard_map/cond/branch_1_fun/ppermute | solution.py:29
  209.4 40.7 %collective-permute-start.41 = (bf16[64,4096]{1,0:T(8,128)(2,1)}, bf16[64,4096]{1,0:T(8,128)(2,1)}, u32[]{:S(2)}, u32[]{:S(2)}) collective-permute-start(bf16[64,4096]{1,0:T(8,128)(2,1)} %get-tuple-element.58), channel_id=1, source_target_pairs={{0,6},{1,7},{2,0},{3,1},{4,2},{5,3},{6,4},{7,5},{8,14},{9,15},{10,... | collective-permute-start | bytes 1572872 | tf_op jit(solution)/shard_map/cond/branch_1_fun/ppermute | solution.py:29
  210.7 39.4 %collective-permute-start.40 = (bf16[64,4096]{1,0:T(8,128)(2,1)}, bf16[64,4096]{1,0:T(8,128)(2,1)}, u32[]{:S(2)}, u32[]{:S(2)}) collective-permute-start(bf16[64,4096]{1,0:T(8,128)(2,1)} %get-tuple-element.59), channel_id=1, source_target_pairs={{0,5},{1,6},{2,7},{3,0},{4,1},{5,2},{6,3},{7,4},{8,13},{9,14},{10,... | collective-permute-start | bytes 1572872 | tf_op jit(solution)/shard_map/cond/branch_1_fun/ppermute | solution.py:29
  210.7 39.4 %collective-permute-start.39 = (bf16[64,4096]{1,0:T(8,128)(2,1)}, bf16[64,4096]{1,0:T(8,128)(2,1)}, u32[]{:S(2)}, u32[]{:S(2)}) collective-permute-start(bf16[64,4096]{1,0:T(8,128)(2,1)} %get-tuple-element.60), channel_id=1, source_target_pairs={{0,4},{1,5},{2,6},{3,7},{4,0},{5,1},{6,2},{7,3},{8,12},{9,13},{10,... | collective-permute-start | bytes 1572872 | tf_op jit(solution)/shard_map/cond/branch_1_fun/ppermute | solution.py:29
  222.6 33.7 %collective-permute-start.38 = (bf16[64,4096]{1,0:T(8,128)(2,1)S(1)}, bf16[64,4096]{1,0:T(8,128)(2,1)}, u32[]{:S(2)}, u32[]{:S(2)}) collective-permute-start(bf16[64,4096]{1,0:T(8,128)(2,1)S(1)} %get-tuple-element.61), channel_id=1, source_target_pairs={{0,3},{1,4},{2,5},{3,6},{4,7},{5,0},{6,1},{7,2},{8,11},{9,12},{10,... | collective-permute-start | bytes 1572872 | tf_op jit(solution)/shard_map/cond/branch_1_fun/ppermute | solution.py:29
  224.1 32.3 %collective-permute-start.37 = (bf16[64,4096]{1,0:T(8,128)(2,1)S(1)}, bf16[64,4096]{1,0:T(8,128)(2,1)}, u32[]{:S(2)}, u32[]{:S(2)}) collective-permute-start(bf16[64,4096]{1,0:T(8,128)(2,1)S(1)} %get-tuple-element.62), channel_id=1, source_target_pairs={{0,2},{1,3},{2,4},{3,5},{4,6},{5,7},{6,0},{7,1},{8,10},{9,11},{10,... | collective-permute-start | bytes 1572872 | tf_op jit(solution)/shard_map/cond/branch_1_fun/ppermute | solution.py:29
